TPU v7x, 256 devices: a whole 4x4x8 slice. The times are simulated.
256 devices in a mesh: dp: 16 (over z, core), vocab: 16 (over x, y).
Axes of the slice: x: 4, y: 4, z: 8, core: 2. Of those that a mesh axis runs over, the one named last changes fastest.
Arguments:
- hidden: bfloat16 [4096, 4096], P('dp')
- table: bfloat16 [16384, 4096], P(('vocab', 'dp')), as said below
- targets: int32 [4096], P('dp'), may hold values from 0 to 16383
- token_scale: float32 [4096], P('dp'), may hold values from 2 to 32
- enc_ids: int32 [4096], P(('dp', 'vocab')), may hold values from 0 to 16383
- enc_cot: bfloat16 [4096, 4096], P(('dp', 'vocab')), may hold values from -6 to 6
- dec_ids: int32 [4096], P(('dp', 'vocab')), may hold values from 0 to 16383
- dec_cot: bfloat16 [4096, 4096], P(('dp', 'vocab')), may hold values from -6 to 6
Outputs:
- grad_hidden: bfloat16 [4096, 4096], P('dp', 'vocab')
- grad_table: float32 [16384, 4096], P(('vocab', 'dp'))
- loss: float32 [4096], P('dp')
Inputs may be any that keep to these rules, and one draw needn't show every extreme that they name: table entries of order 3 / sqrt(4096).
All inputs are finite; a program needn't handle non-finite values.
Results may differ from a plain program's by a relative error of at most 0.018.
Values may be sent and summed in bfloat16 or wider, within the bound.
No kernel may reach another device: no remote copies, remote signals or barrier semaphores. Data moves between devices by JAX's collectives and lax.ppermute only.
A program may use at most 128 MiB of HBM per device.

v0:
```python
import jax
import jax.numpy as jnp
from jax import lax
from jax.sharding import PartitionSpec as P


def shards(hidden, table, targets, token_scale, enc_ids, enc_cot, dec_ids, dec_cot):
    vocab_rows = table.shape[0] * lax.axis_size("dp")
    offset = lax.axis_index("vocab") * vocab_rows
    gathered = lax.all_gather(table, "dp", axis=0, tiled=True)
    logits = jnp.dot(hidden, gathered.T, preferred_element_type=jnp.float32)
    local_target = targets - offset
    columns = jnp.arange(vocab_rows, dtype=jnp.int32)
    matches = columns[None, :] == local_target[:, None]
    target_part = jnp.sum(jnp.where(matches, logits, 0.0), axis=1)
    local_max = jnp.max(logits, axis=1)
    row_max = lax.pmax(local_max, "vocab")
    expo = jnp.exp(logits - row_max[:, None])
    row_sum, target_logit = lax.psum((jnp.sum(expo, axis=1), target_part), "vocab")
    loss = row_max + jnp.log(row_sum) - target_logit
    dlogits = (
        token_scale[:, None] * (expo / row_sum[:, None] - matches.astype(jnp.float32))
    ).astype(jnp.bfloat16)
    state_term = jnp.dot(dlogits, gathered, preferred_element_type=jnp.float32)
    grad_hidden = lax.psum_scatter(
        state_term.astype(jnp.bfloat16), "vocab", scatter_dimension=1, tiled=True
    )
    ids_one, cot_one, ids_two, cot_two = (
        lax.all_gather(enc_ids, "vocab", axis=0, tiled=True),
        lax.all_gather(enc_cot, "vocab", axis=0, tiled=True),
        lax.all_gather(dec_ids, "vocab", axis=0, tiled=True),
        lax.all_gather(dec_cot, "vocab", axis=0, tiled=True),
    )
    all_ids = jnp.concatenate([ids_one, ids_two], axis=0) - offset
    all_cot = jnp.concatenate([cot_one, cot_two], axis=0)
    hits = (columns[:, None] == all_ids[None, :]).astype(jnp.bfloat16)
    looked_up = jnp.dot(hits, all_cot, preferred_element_type=jnp.float32)
    head = lax.dot_general(
        dlogits, hidden, (((0,), (0,)), ((), ())), preferred_element_type=jnp.float32
    )
    grad_table = lax.psum_scatter(
        (head + looked_up).astype(jnp.bfloat16), "dp", scatter_dimension=0, tiled=True
    ).astype(jnp.float32)
    return (grad_hidden, grad_table, loss)


def solution(mesh):
    placed = (
        P("dp", None),
        P(("vocab", "dp"), None),
        P("dp"),
        P("dp"),
        P(("dp", "vocab")),
        P(("dp", "vocab"), None),
        P(("dp", "vocab")),
        P(("dp", "vocab"), None),
    )
    return jax.shard_map(
        shards,
        mesh=mesh,
        in_specs=placed,
        out_specs=(P("dp", "vocab"), P(("vocab", "dp"), None), P("dp")),
        check_vma=False,
    )
```

profile of v0, /device:TPU:32, one launch (start us, length us, event | category | flops | bytes accessed | tf_op | source)
XLA Modules:
  0.0 417.9 jit_solution(18154777926044538096)
XLA Ops:
  7.2 0.7 all-gather.6.cloned.1.call-update
  8.0 0.7 all-gather.8.cloned.1.call-update
  8.7 0.7 all-gather.4.cloned.1.call-update
  9.4 0.0 reduce-scatter.5.cloned.1.call-start
  9.4 1.3 dynamic-slice
  11.4 0.9 dynamic-update-slice.1
  12.2 0.8 dynamic-update-slice
  13.1 16.5 %all-reduce.2 = (s32[256]{0:T(256)S(1)}, s32[256]{0:T(256)S(1)}) all-reduce(s32[256]{0:T(256)S(1)} %dynamic-update-slice.1, s32[256]{0:T(256)S(1)} %dynamic-update-slice), channel_id=1, replica_groups=mesh['dp'=16,'vocab'=16] {'vocab'}, use_global_device_ids=true, to_apply=%add.1 | all-reduce | flops 512 | bytes 4096
  29.5 0.7 broadcast_subtract_fusion
  30.2 32.8 %all-gather.6.cloned.1.call-done = bf16[256,4096]{1,0:T(8,128)(2,1)} async-done(((bf16[16,4096]{1,0:T(8,128)(2,1)}), bf16[256,4096]{1,0:T(8,128)(2,1)}) %all-gather.6.cloned.1.call-update) | async-done | bytes 2097168 | tf_op jit(solution)/shard_map/all_gather | solution.py:30
  63.0 51.8 %all-gather.8.cloned.1.call-done = bf16[256,4096]{1,0:T(8,128)(2,1)} async-done(((bf16[16,4096]{1,0:T(8,128)(2,1)}), bf16[256,4096]{1,0:T(8,128)(2,1)}) %all-gather.8.cloned.1.call-update) | async-done | bytes 2097168 | tf_op jit(solution)/shard_map/all_gather | solution.py:32
  114.8 10.3 %fusion = f32[1024,4096]{1,0:T(8,128)} fusion(bf16[256,4096]{1,0:T(8,128)(2,1)} %all-gather.8.cloned.1.call-done, bf16[256,4096]{1,0:T(8,128)(2,1)} %all-gather.6.cloned.1.call-done, s32[512]{0:T(512)S(1)} %add_subtract_fusion), kind=kOutput, calls=%fused_computation.2 | convolution fusion | flops 4303880192 | bytes 20973568 | tf_op jit(solution)/shard_map/dot_general | solution.py:37
  125.1 45.1 %all-gather.4.cloned.1.call-done = bf16[1024,4096]{1,0:T(8,128)(2,1)} async-done(((bf16[64,4096]{1,0:T(8,128)(2,1)}), bf16[1024,4096]{1,0:T(8,128)(2,1)}) %all-gather.4.cloned.1.call-update) | async-done | bytes 8388624 | tf_op jit(solution)/shard_map/all_gather | solution.py:10
  170.2 5.8 %fusion.7 = (f32[256]{0:T(256)S(1)}, f32[256,1024]{1,0:T(8,128)S(1)}) fusion(bf16[256,4096]{1,0:T(8,128)(2,1)S(1)} %copy-done, bf16[1024,4096]{1,0:T(8,128)(2,1)} %all-gather.4.cloned.1.call-done), kind=kOutput, calls=%fused_computation.17 | convolution fusion | flops 2147745536 | bytes 11535360 | tf_op jit(solution)/shard_map/dot_general | solution.py:11
  176.0 40.3 %pmax.7 = f32[256]{0:T(256)S(1)} all-reduce(f32[256]{0:T(256)S(1)} %get-tuple-element.9), channel_id=1, replica_groups=mesh['dp'=16,'vocab'=16] {'vocab'}, use_global_device_ids=true, to_apply=%region_1.2 | all-reduce | flops 256 | bytes 2048 | tf_op jit(solution)/shard_map/pmax | solution.py:17
  216.4 0.5 select_reduce_fusion
  216.8 35.5 %all-reduce.3 = (f32[256]{0:T(256)S(1)}, f32[256]{0:T(256)S(1)}) all-reduce(f32[256]{0:T(256)S(1)} %get-tuple-element.4, f32[256]{0:T(256)S(1)} %get-tuple-element.3), channel_id=1, replica_groups=mesh['dp'=16,'vocab'=16] {'vocab'}, use_global_device_ids=true, to_apply=%region_3.4 | all-reduce | flops 512 | bytes 4096 | tf_op jit(solution)/shard_map/psum | solution.py:19
  252.3 9.2 %add_convert_fusion = bf16[1024,4096]{1,0:T(8,128)(2,1)} fusion(f32[1024,4096]{1,0:T(8,128)} %fusion, bf16[256,4096]{1,0:T(8,128)(2,1)S(1)} %copy-done, f32[256,1024]{1,0:T(8,128)S(1)} %get-tuple-element.10, s32[256]{0:T(256)S(1)} %broadcast_subtract_fusion, f32[256]{0:T(256)S(1)} %get-tuple-element.7, f32[256]{0:T(256)S(1)} %pmax.7, f32[256]{0:T(256)S(1)} %copy-done.1), kind=kOutput, calls=%fused_computation | convolution fusion | flops 2157707264 | bytes 28315648 | tf_op jit(solution)/shard_map/dot_general | solution.py:38
  261.5 0.0 reduce-scatter.3.cloned.1.call-start
  261.6 7.4 %convolution_convert_fusion = bf16[256,4096]{1,0:T(8,128)(2,1)} fusion(bf16[1024,4096]{1,0:T(8,128)(2,1)} %all-gather.4.cloned.1.call-done, f32[256,1024]{1,0:T(8,128)S(1)} %get-tuple-element.10, s32[256]{0:T(256)S(1)} %broadcast_subtract_fusion, f32[256]{0:T(256)S(1)} %get-tuple-element.7, f32[256]{0:T(256)S(1)} %pmax.7, f32[256]{0:T(256)S(1)} %copy-done.1), kind=kOutput, calls=%fused_computation.1 | convolution fusion | flops 2150367232 | bytes 11538432 | tf_op jit(solution)/shard_map/dot_general | solution.py:24
  269.0 0.6 add_subtract_fusion.1
  269.5 56.1 %reduce-scatter.5.cloned.1.call-done = bf16[64,4096]{1,0:T(8,128)(2,1)} async-done(((bf16[1024,4096]{1,0:T(8,128)(2,1)}), bf16[64,4096]{1,0:T(8,128)(2,1)}) %reduce-scatter.5.cloned.1.call-update) | async-done | bytes 524304 | tf_op jit(solution)/shard_map/reduce_scatter | solution.py:41
  325.6 2.1 convert_element_type.20
  327.7 83.7 %reduce-scatter.3.cloned.1.call-done = bf16[256,256]{1,0:T(8,128)(2,1)} async-done(((bf16[256,4096]{1,0:T(8,128)(2,1)}), bf16[256,256]{1,0:T(8,128)(2,1)}) %reduce-scatter.3.cloned.1.call-update) | async-done | bytes 131088 | tf_op jit(solution)/shard_map/reduce_scatter | solution.py:25
  (12 shorter events, 0.2 us)
Async XLA Ops:
  7.2 163.1 %copy-start = (bf16[256,4096]{1,0:T(8,128)(2,1)S(1)}, bf16[256,4096]{1,0:T(8,128)(2,1)}, u32[]{:S(2)}) copy-start(bf16[256,4096]{1,0:T(8,128)(2,1)} %param.8) | copy-start | bytes 6291460
  7.2 55.8 %all-gather.6.cloned.1.call-start = ((), (), s32[]{:S(2)}) async-start(), calls=%async_computation.4 | async-start | bytes 2228224 | tf_op jit(solution)/shard_map/all_gather | solution.py:30
  7.9 106.9 %all-gather.8.cloned.1.call-start = ((), (), s32[]{:S(2)}) async-start(), calls=%async_computation.5 | async-start | bytes 2228224 | tf_op jit(solution)/shard_map/all_gather | solution.py:32
  8.7 161.5 %all-gather.4.cloned.1.call-start = ((), (), s32[]{:S(2)}) async-start(), calls=%async_computation.2 | async-start | bytes 8912896 | tf_op jit(solution)/shard_map/all_gather | solution.py:10
  9.4 316.2 %reduce-scatter.5.cloned.1.call-start = ((), (), s32[]{:S(2)}) async-start(), calls=%async_computation.6 | async-start | bytes 8912896 | tf_op jit(solution)/shard_map/reduce_scatter | solution.py:41
  125.1 127.2 %copy-start.1 = (f32[256]{0:T(256)S(1)}, f32[256]{0:T(256)}, u32[]{:S(2)}) copy-start(f32[256]{0:T(256)} %param.11) | copy-start | bytes 3076
  261.5 149.9 %reduce-scatter.3.cloned.1.call-start = ((), (), s32[]{:S(2)}) async-start(), calls=%async_computation.3 | async-start | bytes 2228224 | tf_op jit(solution)/shard_map/reduce_scatter | solution.py:25
Sparse Core Ops, SparseCore 0:
  10.4 52.5 all-gather.5
  65.5 49.3 all-gather.7
  116.7 53.4 all-gather.3
  261.6 63.9 reduce-scatter.4
  329.6 81.7 reduce-scatter.2
where the time goes:
time: 418 us
  waiting for transfers between devices  272 us (65%)
  blocking collectives  92.2 us (22%)
  matrix products  32.7 us (8%)
  between operations  14.5 us (3%)
    reduce_scatter x1, waiting for transfers between devices, shards(): lax.psum_scatter(state_term.astype(jnp.bfloat16), 'vocab', scatter_dimens...  83.7 us
    reduce_scatter x1, waiting for transfers between devices, shards(): lax.psum_scatter((head + looked_up).astype(jnp.bfloat16), 'dp', scatter_d...  56.1 us
    all_gather x1, waiting for transfers between devices, shards(): lax.all_gather(dec_cot, 'vocab', axis=0, tiled=True)  51.8 us
    all_gather x1, waiting for transfers between devices, shards(): gathered = lax.all_gather(table, 'dp', axis=0, tiled=True)  45.1 us
    pmax x1, blocking collectives, shards(): row_max = lax.pmax(local_max, 'vocab')  40.3 us
    psum x1, blocking collectives, shards(): lax.psum((jnp.sum(expo, axis=1), target_part), 'vocab')  35.5 us
    all_gather x1, waiting for transfers between devices, shards(): lax.all_gather(enc_cot, 'vocab', axis=0, tiled=True)  32.8 us
    unnamed x1, blocking collectives  16.5 us
  transfers between devices with their start and end apart: 5, of which 5 were waited for; matrix products, arithmetic and copies ran while one was open for 6% of the time, Pallas kernels for 0%

commit v1 on v0

--- a/solution.py
+++ b/solution.py
@@ -7,7 +7,9 @@
 def shards(hidden, table, targets, token_scale, enc_ids, enc_cot, dec_ids, dec_cot):
     vocab_rows = table.shape[0] * lax.axis_size("dp")
     offset = lax.axis_index("vocab") * vocab_rows
-    gathered = lax.all_gather(table, "dp", axis=0, tiled=True)
+    gathered = jnp.concatenate(
+        lax.all_to_all(jnp.stack([table] * lax.axis_size("dp")), "dp", 0, 0), axis=0
+    )
     logits = jnp.dot(hidden, gathered.T, preferred_element_type=jnp.float32)
     local_target = targets - offset
     columns = jnp.arange(vocab_rows, dtype=jnp.int32)

time: 418 us -> 452 us (1.081)
  waiting for transfers between devices: 272 us -> 294 us
  starting transfers between devices: 0.19 us -> 8.88 us
    all_to_all x0 -> x1, waiting for transfers between devices: none -> 65.8 us  [shards(): lax.all_to_all(jnp.stack([table] * lax.axis_size('dp')), 'dp', 0, 0)]
    all_gather x1 -> x0, waiting for transfers between devices: 45.1 us -> none  [shards(): gathered = lax.all_gather(table, 'dp', axis=0, tiled=True)]
    all_to_all x0 -> x1, starting transfers between devices: none -> 8.73 us  [shards(): lax.all_to_all(jnp.stack([table] * lax.axis_size('dp')), 'dp', 0, 0)]
    another operation x0 -> x1, local copies, waits for them, and re-layouts: none -> 5.47 us  [shards(): jnp.stack([table] * lax.axis_size('dp'))]
  transfers between devices with their start and end apart: 5 -> 5, of which waited for: 5 -> 5; matrix products, arithmetic and copies ran while one was open for 6% -> 5% of each run, Pallas kernels for 0% -> 0%
where the time goes in v1:
time: 452 us
  waiting for transfers between devices  294 us (65%)
  blocking collectives  92.6 us (20%)
  matrix products  32.7 us (7%)
  between operations  14.5 us (3%)
  starting transfers between devices  8.88 us (2%)
  local copies, waits for them, and re-layouts  6.55 us (1%)
    reduce_scatter x1, waiting for transfers between devices, shards(): lax.psum_scatter(state_term.astype(jnp.bfloat16), 'vocab', scatter_dimens...  83.7 us
    all_to_all x1, waiting for transfers between devices, shards(): lax.all_to_all(jnp.stack([table] * lax.axis_size('dp')), 'dp', 0, 0)  65.8 us
    reduce_scatter x1, waiting for transfers between devices, shards(): lax.psum_scatter((head + looked_up).astype(jnp.bfloat16), 'dp', scatter_d...  56.1 us
    all_gather x1, waiting for transfers between devices, shards(): lax.all_gather(dec_cot, 'vocab', axis=0, tiled=True)  51.8 us
    pmax x1, blocking collectives, shards(): row_max = lax.pmax(local_max, 'vocab')  40.7 us
    psum x1, blocking collectives, shards(): lax.psum((jnp.sum(expo, axis=1), target_part), 'vocab')  35.5 us
    all_gather x1, waiting for transfers between devices, shards(): lax.all_gather(enc_cot, 'vocab', axis=0, tiled=True)  34.7 us
    unnamed x1, blocking collectives  16.5 us
  transfers between devices with their start and end apart: 5, of which 5 were waited for; matrix products, arithmetic and copies ran while one was open for 5% of the time, Pallas kernels for 0%

profile of v1, /device:TPU:32, one launch (start us, length us, event | category | flops | bytes accessed | tf_op | source)
XLA Modules:
  0.0 451.9 jit_solution(7261879827952441077)
XLA Ops:
  7.2 5.5 %stack.2 = bf16[16,64,4096]{2,1,0:T(8,128)(2,1)} broadcast(bf16[64,4096]{1,0:T(8,128)(2,1)} %param.9), dimensions={1,2} | broadcast | bytes 8912896 | tf_op jit(solution)/shard_map/stack | solution.py:11
  12.7 8.7 %all-to-all-start = ((bf16[16,64,4096]{2,1,0:T(8,128)(2,1)}), bf16[16,64,4096]{2,1,0:T(8,128)(2,1)}, u32[]{:S(2)}, u32[]{:S(2)}) async-start(bf16[16,64,4096]{2,1,0:T(8,128)(2,1)} %stack.2), calls=%async_computation | async-start | bytes 16777216 | tf_op jit(solution)/shard_map/all_to_all | solution.py:11
  21.4 0.7 all-gather.3.cloned.1.call-update
  22.2 0.7 all-gather.5.cloned.1.call-update
  22.9 0.0 reduce-scatter.5.cloned.1.call-start
  22.9 0.6 dynamic-slice
  24.2 0.2 dynamic-update-slice.1
  24.4 0.2 dynamic-update-slice
  24.7 16.5 %all-reduce.2 = (s32[256]{0:T(256)S(1)}, s32[256]{0:T(256)S(1)}) all-reduce(s32[256]{0:T(256)S(1)} %dynamic-update-slice.1, s32[256]{0:T(256)S(1)} %dynamic-update-slice), channel_id=1, replica_groups=mesh['dp'=16,'vocab'=16] {'vocab'}, use_global_device_ids=true, to_apply=%add.1 | all-reduce | flops 512 | bytes 4096
  41.1 34.7 %all-gather.3.cloned.1.call-done = bf16[256,4096]{1,0:T(8,128)(2,1)} async-done(((bf16[16,4096]{1,0:T(8,128)(2,1)}), bf16[256,4096]{1,0:T(8,128)(2,1)}) %all-gather.3.cloned.1.call-update) | async-done | bytes 2097168 | tf_op jit(solution)/shard_map/all_gather | solution.py:32
  75.9 51.8 %all-gather.5.cloned.1.call-done = bf16[256,4096]{1,0:T(8,128)(2,1)} async-done(((bf16[16,4096]{1,0:T(8,128)(2,1)}), bf16[256,4096]{1,0:T(8,128)(2,1)}) %all-gather.5.cloned.1.call-update) | async-done | bytes 2097168 | tf_op jit(solution)/shard_map/all_gather | solution.py:34
  127.7 10.3 %fusion = f32[1024,4096]{1,0:T(8,128)} fusion(bf16[256,4096]{1,0:T(8,128)(2,1)} %all-gather.5.cloned.1.call-done, bf16[256,4096]{1,0:T(8,128)(2,1)} %all-gather.3.cloned.1.call-done, s32[512]{0:T(512)S(1)} %add_subtract_fusion), kind=kOutput, calls=%fused_computation.2 | convolution fusion | flops 4303880192 | bytes 20973568 | tf_op jit(solution)/shard_map/dot_general | solution.py:39
  138.0 65.8 %all-to-all-done = bf16[16,64,4096]{2,1,0:T(8,128)(2,1)} async-done(((bf16[16,64,4096]{2,1,0:T(8,128)(2,1)}), bf16[16,64,4096]{2,1,0:T(8,128)(2,1)}, u32[]{:S(2)}, u32[]{:S(2)}) %all-to-all-start) | async-done | bytes 8388640 | tf_op jit(solution)/shard_map/all_to_all | solution.py:11
  203.8 5.8 %fusion.7 = (f32[256]{0:T(256)S(1)}, f32[256,1024]{1,0:T(8,128)S(1)}) fusion(bf16[256,4096]{1,0:T(8,128)(2,1)S(1)} %copy-done, bf16[1024,4096]{1,0:T(8,128)(2,1)} %bitcast), kind=kOutput, calls=%fused_computation.17 | convolution fusion | flops 2147745536 | bytes 11535360 | tf_op jit(solution)/shard_map/dot_general | solution.py:13
  209.6 40.7 %pmax.7 = f32[256]{0:T(256)S(1)} all-reduce(f32[256]{0:T(256)S(1)} %get-tuple-element.9), channel_id=1, replica_groups=mesh['dp'=16,'vocab'=16] {'vocab'}, use_global_device_ids=true, to_apply=%region_1.2 | all-reduce | flops 256 | bytes 2048 | tf_op jit(solution)/shard_map/pmax | solution.py:19
  250.3 0.5 select_reduce_fusion
  250.8 35.5 %all-reduce.3 = (f32[256]{0:T(256)S(1)}, f32[256]{0:T(256)S(1)}) all-reduce(f32[256]{0:T(256)S(1)} %get-tuple-element.4, f32[256]{0:T(256)S(1)} %get-tuple-element.3), channel_id=1, replica_groups=mesh['dp'=16,'vocab'=16] {'vocab'}, use_global_device_ids=true, to_apply=%region_3.4 | all-reduce | flops 512 | bytes 4096 | tf_op jit(solution)/shard_map/psum | solution.py:21
  286.2 9.2 %add_convert_fusion = bf16[1024,4096]{1,0:T(8,128)(2,1)} fusion(f32[1024,4096]{1,0:T(8,128)} %fusion, bf16[256,4096]{1,0:T(8,128)(2,1)S(1)} %copy-done, f32[256,1024]{1,0:T(8,128)S(1)} %get-tuple-element.10, s32[256]{0:T(256)S(1)} %broadcast_subtract_fusion, f32[256]{0:T(256)S(1)} %get-tuple-element.7, f32[256]{0:T(256)S(1)} %pmax.7, f32[256]{0:T(256)S(1)} %copy-done.1), kind=kOutput, calls=%fused_computation | convolution fusion | flops 2157707264 | bytes 28315648 | tf_op jit(solution)/shard_map/dot_general | solution.py:40
  295.5 0.0 reduce-scatter.3.cloned.1.call-start
  295.5 7.4 %convolution_convert_fusion = bf16[256,4096]{1,0:T(8,128)(2,1)} fusion(bf16[1024,4096]{1,0:T(8,128)(2,1)} %bitcast, f32[256,1024]{1,0:T(8,128)S(1)} %get-tuple-element.10, s32[256]{0:T(256)S(1)} %broadcast_subtract_fusion, f32[256]{0:T(256)S(1)} %get-tuple-element.7, f32[256]{0:T(256)S(1)} %pmax.7, f32[256]{0:T(256)S(1)} %copy-done.1), kind=kOutput, calls=%fused_computation.1 | convolution fusion | flops 2150367232 | bytes 11538432 | tf_op jit(solution)/shard_map/dot_general | solution.py:26
  302.9 0.6 add_subtract_fusion.1
  303.5 56.1 %reduce-scatter.5.cloned.1.call-done = bf16[64,4096]{1,0:T(8,128)(2,1)} async-done(((bf16[1024,4096]{1,0:T(8,128)(2,1)}), bf16[64,4096]{1,0:T(8,128)(2,1)}) %reduce-scatter.5.cloned.1.call-update) | async-done | bytes 524304 | tf_op jit(solution)/shard_map/reduce_scatter | solution.py:43
  359.6 2.1 convert_element_type.20
  361.7 83.7 %reduce-scatter.3.cloned.1.call-done = bf16[256,256]{1,0:T(8,128)(2,1)} async-done(((bf16[256,4096]{1,0:T(8,128)(2,1)}), bf16[256,256]{1,0:T(8,128)(2,1)}) %reduce-scatter.3.cloned.1.call-update) | async-done | bytes 131088 | tf_op jit(solution)/shard_map/reduce_scatter | solution.py:27
  (20 shorter events, 0.2 us)
Async XLA Ops:
  7.2 196.6 %copy-start = (bf16[256,4096]{1,0:T(8,128)(2,1)S(1)}, bf16[256,4096]{1,0:T(8,128)(2,1)}, u32[]{:S(2)}) copy-start(bf16[256,4096]{1,0:T(8,128)(2,1)} %param.8) | copy-start | bytes 6291460
  12.6 10.3 %copy-start.5 = (u32[256]{0:T(256)S(1)}, u32[256]{0:T(256)}, u32[]{:S(2)}) copy-start(u32[256]{0:T(256)} %constant.17) | copy-start | bytes 3076
  12.6 11.5 %copy-start.3 = (s32[16]{0:T(128)S(1)}, s32[16]{0:T(128)}, u32[]{:S(2)}) copy-start(s32[16]{0:T(128)} %param.14) | copy-start | bytes 196
  12.7 11.8 %copy-start.4 = (s32[16]{0:T(128)S(1)}, s32[16]{0:T(128)}, u32[]{:S(2)}) copy-start(s32[16]{0:T(128)} %param.12) | copy-start | bytes 196
  12.7 28.5 %copy-start.2 = (s32[256]{0:T(256)S(1)}, s32[256]{0:T(256)}, u32[]{:S(2)}) copy-start(s32[256]{0:T(256)} %param.10) | copy-start | bytes 3076
  12.7 191.1 %all-to-all-start = ((bf16[16,64,4096]{2,1,0:T(8,128)(2,1)}), bf16[16,64,4096]{2,1,0:T(8,128)(2,1)}, u32[]{:S(2)}, u32[]{:S(2)}) async-start(bf16[16,64,4096]{2,1,0:T(8,128)(2,1)} %stack.2), calls=%async_computation | async-start | bytes 16777216 | tf_op jit(solution)/shard_map/all_to_all | solution.py:11
  21.4 54.5 %all-gather.3.cloned.1.call-start = ((), (), s32[]{:S(2)}) async-start(), calls=%async_computation.4 | async-start | bytes 2228224 | tf_op jit(solution)/shard_map/all_gather | solution.py:32
  22.1 105.6 %all-gather.5.cloned.1.call-start = ((), (), s32[]{:S(2)}) async-start(), calls=%async_computation.5 | async-start | bytes 2228224 | tf_op jit(solution)/shard_map/all_gather | solution.py:34
  22.9 336.7 %reduce-scatter.5.cloned.1.call-start = ((), (), s32[]{:S(2)}) async-start(), calls=%async_computation.6 | async-start | bytes 8912896 | tf_op jit(solution)/shard_map/reduce_scatter | solution.py:43
  203.8 82.4 %copy-start.1 = (f32[256]{0:T(256)S(1)}, f32[256]{0:T(256)}, u32[]{:S(2)}) copy-start(f32[256]{0:T(256)} %param.11) | copy-start | bytes 3076
  295.5 149.9 %reduce-scatter.3.cloned.1.call-start = ((), (), s32[]{:S(2)}) async-start(), calls=%async_computation.3 | async-start | bytes 2228224 | tf_op jit(solution)/shard_map/reduce_scatter | solution.py:27
Sparse Core Ops, SparseCore 0:
  24.7 51.1 all-gather.2
  78.3 49.3 all-gather.4
  295.6 63.9 reduce-scatter.4
  363.6 81.7 reduce-scatter.2
